TPU v7x, 32 devices: a whole 2x2x4 slice. The times are simulated.
32 devices in a mesh: hap: 2 (over x), snp: 16 (over z, y, core).
Axes of the slice: x: 2, y: 2, z: 4, core: 2. Of those that a mesh axis runs over, the one named last changes fastest.
Arguments:
- packed_panel: int32 [96, 16384], P('hap', 'snp'), may hold values from 0 to 8191, as said below
- components: bfloat16 [64, 1248], P(None, 'hap'), may hold values from -0.15625 to 0.15625
- bounds: int32 [2, 16384], P(None, 'snp'), may hold values from 0 to 16383, as said below
- band_width: int32 [16384], P('snp'), may hold values from 1 to 256
Outputs:
- ld_scores: float32 [16384], P('snp')
Inputs may be any that keep to these rules, and one draw needn't show every extreme that they name: Bit j of packed_panel[w, s] (j from 0 to 12) is the allele of haplotype 13 w + j at SNP s; higher bits are zero. LD blocks are consecutive runs of 1 to 2048 SNPs that cover all SNPs in order; bounds[0, s] and bounds[1, s] are the first and last SNP of the block holding s.
All inputs are finite; a program needn't handle non-finite values.
Results may differ from a plain program's by a relative error of at most 0.00074.
Values may be sent and summed in bfloat16 or wider, within the bound.
No kernel may reach another device: no remote copies, remote signals or barrier semaphores. Data moves between devices by JAX's collectives and lax.ppermute only.
A program may use at most 64 MiB of HBM per device.

v0:
```python
import jax
import jax.numpy as jnp
from jax import lax
from jax.sharding import PartitionSpec as P

epsilon = 1e-06


def padded_2(block, sides, width):
    for axis, dim in sides:
        count = lax.axis_size(axis)
        forward = [(i, i + 1) for i in range(count - 1)]
        backward = [(target, source) for source, target in forward]
        low = lax.ppermute(
            lax.slice_in_dim(block, block.shape[dim] - width, None, axis=dim), axis, forward
        )
        high = lax.ppermute(lax.slice_in_dim(block, 0, width, axis=dim), axis, backward)
        block = jnp.concatenate([low, block, high], axis=dim)
    return block


def unpack(packed):
    shifts = jnp.arange(13, dtype=jnp.int32)
    bit_values = jnp.bitwise_and(jnp.right_shift(packed[:, None, :], shifts[None, :, None]), 1)
    return bit_values.reshape(packed.shape[0] * 13, packed.shape[1]).astype(jnp.bfloat16)


def project(components, packed_panel):
    column_count = packed_panel.shape[1]
    block_size = min(256, column_count)
    zeroed = jnp.zeros((components.shape[0], column_count), jnp.float32)

    def add_block(block_index, accumulated):
        packed = lax.dynamic_slice_in_dim(packed_panel, block_index * block_size, block_size, 1)
        product = jnp.dot(components, unpack(packed), preferred_element_type=jnp.float32)
        return lax.dynamic_update_slice_in_dim(accumulated, product, block_index * block_size, 1)

    return lax.fori_loop(0, column_count // block_size, add_block, zeroed)


def standardize(factor):
    average = jnp.mean(factor, axis=1, keepdims=True)
    centered = factor - average
    variance = jnp.mean(centered * centered, axis=1, keepdims=True)
    return (centered * lax.rsqrt(variance + epsilon)).astype(jnp.bfloat16)


def band_scores(padded, inverse, bounds, band_width, offset, start_row, row_count, reach_width):
    component_count = padded.shape[0]
    block_size = min(256, row_count)

    def block_scores(block_index):
        first_row = start_row + block_index * block_size
        row_part = lax.dynamic_slice_in_dim(padded, first_row + reach_width, block_size, 1)
        column_part = lax.dynamic_slice_in_dim(padded, first_row, block_size + 2 * reach_width, 1)
        inverse_rows = lax.dynamic_slice_in_dim(inverse, first_row + reach_width, block_size, 0)
        inverse_columns = lax.dynamic_slice_in_dim(
            inverse, first_row, block_size + 2 * reach_width, 0
        )
        block_first = lax.dynamic_slice_in_dim(bounds[0], first_row, block_size, 0)
        block_last = lax.dynamic_slice_in_dim(bounds[1], first_row, block_size, 0)
        row_reach = lax.dynamic_slice_in_dim(band_width, first_row, block_size, 0)
        inner_products = lax.dot_general(
            row_part, column_part, (((0,), (0,)), ((), ())), preferred_element_type=jnp.float32
        )
        correlation = (
            inner_products
            * (1.0 / component_count)
            * inverse_rows[:, None]
            * inverse_columns[None, :]
        )
        row_position = offset + first_row + jnp.arange(block_size, dtype=jnp.int32)
        column_position = (
            offset
            + first_row
            - reach_width
            + jnp.arange(block_size + 2 * reach_width, dtype=jnp.int32)
        )
        window_low = jnp.maximum(block_first, row_position - row_reach)
        window_high = jnp.minimum(block_last, row_position + row_reach)
        inside = (
            (column_position[None, :] >= window_low[:, None])
            & (column_position[None, :] <= window_high[:, None])
            & (column_position[None, :] != row_position[:, None])
        )
        squared_sum = jnp.sum(jnp.where(inside, correlation * correlation, 0.0), axis=1)
        window_count = jnp.sum(inside.astype(jnp.float32), axis=1)
        return component_count * squared_sum / jnp.maximum(window_count, 1.0)

    blocks = jnp.arange(row_count // block_size, dtype=jnp.int32)
    return lax.map(block_scores, blocks).reshape(row_count)


def on_device(packed_panel, components, bounds, band_width):
    partial_factor = project(components, packed_panel)
    column_count = partial_factor.shape[1]
    factor = lax.psum(partial_factor, "hap")
    component_rows = lax.all_to_all(factor, "snp", split_axis=0, concat_axis=1, tiled=True)
    scaled = standardize(component_rows)
    normed = lax.all_to_all(scaled, "snp", split_axis=1, concat_axis=0, tiled=True)
    reach_width = column_count // 4
    padded = padded_2(normed, (("snp", 1),), reach_width)
    inverse = lax.rsqrt(jnp.mean(jnp.square(padded.astype(jnp.float32)), axis=0) + epsilon)
    offset = lax.axis_index("snp") * column_count
    share_rows = column_count // lax.axis_size("hap")
    own_scores = band_scores(
        padded,
        inverse,
        bounds,
        band_width,
        offset,
        lax.axis_index("hap") * share_rows,
        share_rows,
        reach_width,
    )
    return lax.all_gather(own_scores, "hap", axis=0, tiled=True)


def solution(mesh):
    in_specs = (P("hap", "snp"), P(None, "hap"), P(None, "snp"), P("snp"))
    out_specs = P("snp")
    return jax.shard_map(
        on_device, mesh=mesh, in_specs=in_specs, out_specs=out_specs, check_vma=False
    )
```

profile of v0, /device:TPU:13, one launch (start us, length us, event | category | flops | bytes accessed | tf_op | source)
XLA Modules:
  0.0 91.0 jit_solution(2346714453307130350)
XLA Ops:
  6.6 0.9 copy-done
  7.4 5.6 %while.25 = (s32[]{:T(128)}, f32[64,1024]{1,0:T(8,128)S(1)}, s32[48,1024]{1,0:T(8,128)}, bf16[64,624]{1,0:T(8,128)(2,1)S(1)}, s32[]{:T(128)}, /*index=5*/s32[]{:T(128)}, s32[]{:T(128)}, s32[]{:T(128)}) while((s32[]{:T(128)}, f32[64,1024]{1,0:T(8,128)S(1)}, s32[48,1024]{1,0:T(8,128)}, bf16[64,624]{1,0:T(8,128)(2,1)S(1)}, s32[]{:T(128)}, ...), condition=%wide.region_1.0_spmd, body=%wide.region_0.0_spmd.sunk | while | flops 20926468 | bytes 2862539 | solution.py:38
  7.4 0.8 constant_dynamic-slice_fusion.6
  8.2 0.1 shift_right_arithmetic.50
  8.3 0.1 shift_right_arithmetic.51
  8.4 0.1 shift_right_arithmetic.53
  8.5 0.3 fusion.22
  8.8 0.8 constant_dynamic-slice_fusion.6
  9.6 0.1 shift_right_arithmetic.50
  9.7 0.1 shift_right_arithmetic.51
  9.8 0.1 shift_right_arithmetic.53
  9.9 0.3 fusion.22
  10.3 0.8 constant_dynamic-slice_fusion.6
  11.1 0.1 shift_right_arithmetic.50
  11.1 0.1 shift_right_arithmetic.51
  11.2 0.1 shift_right_arithmetic.53
  11.4 0.3 fusion.22
  11.7 0.8 constant_dynamic-slice_fusion.6
  12.5 0.1 shift_right_arithmetic.50
  12.5 0.1 shift_right_arithmetic.51
  12.6 0.1 shift_right_arithmetic.53
  12.8 0.3 fusion.22
  13.1 0.8 all_to_all.22
  13.9 24.1 %all-reduce.2.cloned.1.call-done = f32[16,4,1024]{2,1,0:T(4,128)} async-done(((f32[16,4,1024]{2,1,0:T(4,128)}), f32[16,4,1024]{2,1,0:T(4,128)}) %all-reduce.2.cloned.1.call-update) | async-done | bytes 262160 | tf_op jit(solution)/shard_map/psum | solution.py:97
  37.9 14.8 %all_to_all.29 = f32[16,4,1024]{2,1,0:T(4,128)S(1)} all-to-all(f32[16,4,1024]{2,1,0:T(4,128)} %all-reduce.2.cloned.1.call-done), channel_id=1, replica_groups=mesh['hap'=2,'snp'=16] {'snp'}, dimensions={0} | all-to-all | bytes 524288 | tf_op jit(solution)/shard_map/all_to_all | solution.py:98
  52.7 0.3 reduce_sum.51
  53.0 0.3 multiply_reduce_fusion.1
  53.3 0.1 fusion.11
  53.5 9.9 %all_to_all.30 = bf16[4,16,1024]{2,0,1:T(4,128)(2,1)S(1)} all-to-all(bf16[4,16,1024]{2,0,1:T(4,128)(2,1)S(1)} %fusion.11), channel_id=1, replica_groups=mesh['hap'=2,'snp'=16] {'snp'}, dimensions={1} | all-to-all | bytes 262144 | tf_op jit(solution)/shard_map/all_to_all | solution.py:100
  63.4 3.7 %collective-permute-start = (bf16[64,256]{1,0:T(8,128)(2,1)S(1)}, bf16[64,256]{1,0:T(8,128)(2,1)S(1)}, u32[]{:S(2)}, u32[]{:S(2)}) collective-permute-start(bf16[64,256]{1,0:T(8,128)(2,1)S(1)} %get-tuple-element.232), channel_id=1, source_target_pairs={{0,1},{1,2},{2,3},{3,4},{4,5},{5,6},{6,7},{7,8},{8,9},{9,10},{10,1... | collective-permute-start | bytes 98312 | tf_op jit(solution)/shard_map/ppermute | solution.py:14
  67.1 1.9 %collective-permute-start.1 = (bf16[64,256]{1,0:T(8,128)(2,1)S(1)}, bf16[64,256]{1,0:T(8,128)(2,1)S(1)}, u32[]{:S(2)}, u32[]{:S(2)}) collective-permute-start(bf16[64,256]{1,0:T(8,128)(2,1)S(1)} %get-tuple-element.231), channel_id=1, source_target_pairs={{1,0},{2,1},{3,2},{4,3},{5,4},{6,5},{7,6},{8,7},{9,8},{10,9},{11,1... | collective-permute-start | bytes 98312 | tf_op jit(solution)/shard_map/ppermute | solution.py:17
  69.1 4.2 %collective-permute-done.1 = bf16[64,256]{1,0:T(8,128)(2,1)S(1)} collective-permute-done((bf16[64,256]{1,0:T(8,128)(2,1)S(1)}, bf16[64,256]{1,0:T(8,128)(2,1)S(1)}, u32[]{:S(2)}, u32[]{:S(2)}) %collective-permute-start.1) | collective-permute-done | bytes 32800 | tf_op jit(solution)/shard_map/ppermute | solution.py:17
  73.4 0.7 copy-done.1
  74.0 6.3 %while.26 = (s32[]{:T(128)}, f32[2,256]{1,0:T(2,128)S(1)}, s32[2]{0:T(128)S(1)}, s32[]{:T(128)}, s32[]{:T(128)}, /*index=5*/s32[2,1024]{1,0:T(2,128)S(1)}, s32[1...) while((s32[]{:T(128)}, f32[2,256]{1,0:T(2,128)S(1)}, ...), condition=%wide.region_9.10_spmd, body=%wide.region_6.9_spmd.sunk | while | flops 28510736 | bytes 194922 | solution.py:91
  74.0 0.6 dynamic_slice.80
  75.4 0.8 subtract_maximum_fusion.2
  76.1 0.1 dynamic-slice_multiply_fusion.2
  76.2 0.1 dynamic_slice.81
  76.3 0.5 fusion.26
  76.8 0.3 convert_reduce_fusion.2
  77.2 0.6 dynamic_slice.80
  78.5 0.8 subtract_maximum_fusion.2
  79.3 0.1 dynamic-slice_multiply_fusion.2
  79.4 0.1 dynamic_slice.81
  79.5 0.5 fusion.26
  80.0 0.3 convert_reduce_fusion.2
  80.4 3.2 %all-gather = f32[2,1,512]{2,1,0:T(1,128)S(1)} all-gather(f32[1,1,512]{2,1,0:T(1,128)S(1)} %reshape.97), channel_id=1, replica_groups=mesh['hap'=2,'snp'=16] {'hap'}, dimensions={0}, use_global_device_ids=true | all-gather | bytes 6144 | tf_op jit(solution)/shard_map/all_gather | solution.py:116
  83.6 0.6 copy.23
  (34 shorter events, 0.4 us)
Async XLA Ops:
  6.5 31.4 %all-reduce.2.cloned.1.call-start = ((), (), s32[]{:S(2)}) async-start(), calls=%async_computation.2 | async-start | bytes 524288 | tf_op jit(solution)/shard_map/psum | solution.py:97
  6.5 0.9 copy-start
  63.4 5.7 %collective-permute-start = (bf16[64,256]{1,0:T(8,128)(2,1)S(1)}, bf16[64,256]{1,0:T(8,128)(2,1)S(1)}, u32[]{:S(2)}, u32[]{:S(2)}) collective-permute-start(bf16[64,256]{1,0:T(8,128)(2,1)S(1)} %get-tuple-element.232), channel_id=1, source_target_pairs={{0,1},{1,2},{2,3},{3,4},{4,5},{5,6},{6,7},{7,8},{8,9},{9,10},{10,1... | collective-permute-start | bytes 98312 | tf_op jit(solution)/shard_map/ppermute | solution.py:14
  67.1 6.1 %collective-permute-start.1 = (bf16[64,256]{1,0:T(8,128)(2,1)S(1)}, bf16[64,256]{1,0:T(8,128)(2,1)S(1)}, u32[]{:S(2)}, u32[]{:S(2)}) collective-permute-start(bf16[64,256]{1,0:T(8,128)(2,1)S(1)} %get-tuple-element.231), channel_id=1, source_target_pairs={{1,0},{2,1},{3,2},{4,3},{5,4},{6,5},{7,6},{8,7},{9,8},{10,9},{11,1... | collective-permute-start | bytes 98312 | tf_op jit(solution)/shard_map/ppermute | solution.py:17
  73.3 0.7 copy-start.1
Sparse Core Ops, SparseCore 0:
  14.0 23.8 all-reduce.1
where the time goes:
time: 91.7 us; the launch traced here: 91 us
  waiting for transfers between devices  28.2 us (31%)
  blocking collectives  27.9 us (30%)
  between operations  13.5 us (15%)
  local copies, waits for them, and re-layouts  8.78 us (10%)
  starting transfers between devices  5.62 us (6%)
  other arithmetic  3.17 us (3%)
  matrix products  2.22 us (2%)
  loops' own time  1.59 us (2%)
    psum x1, waiting for transfers between devices, on_device(): factor = lax.psum(partial_factor, 'hap')  24.1 us
    all_to_all x1, blocking collectives, on_device(): lax.all_to_all(factor, 'snp', split_axis=0, concat_axis=1, tiled=True)  14.8 us
    all_to_all x1, blocking collectives, on_device(): lax.all_to_all(scaled, 'snp', split_axis=1, concat_axis=0, tiled=True)  9.91 us
    ppermute x1, waiting for transfers between devices, padded_2(): lax.ppermute(lax.slice_in_dim(block, 0, width, axis=dim), axis, backward)  4.16 us
    ppermute x1, starting transfers between devices, padded_2(): lax.ppermute(lax.slice_in_dim(block, block.shape[dim] - width, None, axis...  3.7 us
    dynamic_slice x4, local copies, waits for them, and re-layouts, add_block(): lax.dynamic_slice_in_dim(packed_panel, block_index * block_size, block_si...  3.23 us
    all_gather x1, blocking collectives, on_device(): return lax.all_gather(own_scores, 'hap', axis=0, tiled=True)  3.21 us
    unnamed x8, local copies, waits for them, and re-layouts  2.16 us
  transfers between devices with their start and end apart: 3, of which 2 were waited for; matrix products, arithmetic and copies ran while one was open for 0% of the time, Pallas kernels for 0%

commit v1 on v0

--- a/solution.py
+++ b/solution.py
@@ -94,7 +94,7 @@
 def on_device(packed_panel, components, bounds, band_width):
     partial_factor = project(components, packed_panel)
     column_count = partial_factor.shape[1]
-    factor = lax.psum(partial_factor, "hap")
+    factor = jnp.sum(lax.all_gather(partial_factor, "hap"), axis=0)
     component_rows = lax.all_to_all(factor, "snp", split_axis=0, concat_axis=1, tiled=True)
     scaled = standardize(component_rows)
     normed = lax.all_to_all(scaled, "snp", split_axis=1, concat_axis=0, tiled=True)

time: 91.7 us -> 61.7 us (0.67)
  waiting for transfers between devices: 28.2 us -> 4.17 us
  between operations: 13.5 us -> 0.13 us
  blocking collectives: 27.9 us -> 36.1 us
    psum x1 -> x0, waiting for transfers between devices: 24.1 us -> none  [on_device(): factor = lax.psum(partial_factor, 'hap')]
    all_gather x0 -> x1, blocking collectives: none -> 7.85 us  [on_device(): factor = jnp.sum(lax.all_gather(partial_factor, 'hap'), axis=0)]
  transfers between devices with their start and end apart: 3 -> 2, of which waited for: 2 -> 1; matrix products, arithmetic and copies ran while one was open for 0% -> 0% of each run, Pallas kernels for 0% -> 0%
where the time goes in v1:
time: 61.7 us; the launch traced here: 61.1 us
  blocking collectives  36.1 us (59%)
  local copies, waits for them, and re-layouts  8.08 us (13%)
  starting transfers between devices  5.62 us (9%)
  waiting for transfers between devices  4.17 us (7%)
  other arithmetic  3.2 us (5%)
  matrix products  2.22 us (4%)
  loops' own time  1.59 us (3%)
    all_to_all x1, blocking collectives, on_device(): lax.all_to_all(factor, 'snp', split_axis=0, concat_axis=1, tiled=True)  15.1 us
    all_to_all x1, blocking collectives, on_device(): lax.all_to_all(scaled, 'snp', split_axis=1, concat_axis=0, tiled=True)  9.91 us
    all_gather x1, blocking collectives, on_device(): factor = jnp.sum(lax.all_gather(partial_factor, 'hap'), axis=0)  7.85 us
    ppermute x1, waiting for transfers between devices, padded_2(): lax.ppermute(lax.slice_in_dim(block, 0, width, axis=dim), axis, backward)  4.16 us
    ppermute x1, starting transfers between devices, padded_2(): lax.ppermute(lax.slice_in_dim(block, block.shape[dim] - width, None, axis...  3.7 us
    dynamic_slice x4, local copies, waits for them, and re-layouts, add_block(): lax.dynamic_slice_in_dim(packed_panel, block_index * block_size, block_si...  3.23 us
    all_gather x1, blocking collectives, on_device(): return lax.all_gather(own_scores, 'hap', axis=0, tiled=True)  3.21 us
    unnamed x8, local copies, waits for them, and re-layouts  2.16 us
  transfers between devices with their start and end apart: 2, of which 1 were waited for; matrix products, arithmetic and copies ran while one was open for 0% of the time, Pallas kernels for 0%

profile of v1, /device:TPU:13, one launch (start us, length us, event | category | flops | bytes accessed | tf_op | source)
XLA Modules:
  0.0 61.1 jit_solution(8962924693431162730)
XLA Ops:
  0.0 0.9 %copy-done = bf16[64,624]{1,0:T(8,128)(2,1)S(1)} copy-done((bf16[64,624]{1,0:T(8,128)(2,1)S(1)}, bf16[64,624]{1,0:T(8,128)(2,1)}, u32[]{:S(2)}) %copy-start) | copy-done | bytes 79896
  0.9 5.6 %while.25 = (s32[]{:T(128)}, f32[64,1024]{1,0:T(8,128)S(1)}, s32[48,1024]{1,0:T(8,128)}, bf16[64,624]{1,0:T(8,128)(2,1)S(1)}, s32[]{:T(128)}, /*index=5*/s32[]{:T(128)}, s32[]{:T(128)}, s32[]{:T(128)}) while((s32[]{:T(128)}, f32[64,1024]{1,0:T(8,128)S(1)}, s32[48,1024]{1,0:T(8,128)}, bf16[64,624]{1,0:T(8,128)(2,1)S(1)}, s32[]{:T(128)}, ...), condition=%wide.region_1.0_spmd, body=%wide.region_0.0_spmd.sunk | while | flops 20926468 | bytes 2862539 | solution.py:38
  0.9 0.8 %constant_dynamic-slice_fusion.6 = s32[48,256]{1,0:T(8,128)S(1)} fusion(s32[48,1024]{1,0:T(8,128)} %get-tuple-element.341, s32[]{:T(128)S(6)} %select_n.45), kind=kLoop, calls=%fused_computation.5.clone.1 | loop fusion | bytes 98308 | tf_op jit(solution)/shard_map/while/body/eval_jaxpr/dynamic_slice | solution.py:34
  1.7 0.1 shift_right_arithmetic.50
  1.8 0.1 shift_right_arithmetic.51
  1.9 0.1 shift_right_arithmetic.53
  2.0 0.3 fusion.22
  2.3 0.8 %constant_dynamic-slice_fusion.6 = s32[48,256]{1,0:T(8,128)S(1)} fusion(s32[48,1024]{1,0:T(8,128)} %get-tuple-element.341, s32[]{:T(128)S(6)} %select_n.45), kind=kLoop, calls=%fused_computation.5.clone.1 | loop fusion | bytes 98308 | tf_op jit(solution)/shard_map/while/body/eval_jaxpr/dynamic_slice | solution.py:34
  3.1 0.1 shift_right_arithmetic.50
  3.2 0.1 shift_right_arithmetic.51
  3.3 0.1 shift_right_arithmetic.53
  3.4 0.3 fusion.22
  3.7 0.8 %constant_dynamic-slice_fusion.6 = s32[48,256]{1,0:T(8,128)S(1)} fusion(s32[48,1024]{1,0:T(8,128)} %get-tuple-element.341, s32[]{:T(128)S(6)} %select_n.45), kind=kLoop, calls=%fused_computation.5.clone.1 | loop fusion | bytes 98308 | tf_op jit(solution)/shard_map/while/body/eval_jaxpr/dynamic_slice | solution.py:34
  4.5 0.1 shift_right_arithmetic.50
  4.6 0.1 shift_right_arithmetic.51
  4.7 0.1 shift_right_arithmetic.53
  4.8 0.3 fusion.22
  5.1 0.8 %constant_dynamic-slice_fusion.6 = s32[48,256]{1,0:T(8,128)S(1)} fusion(s32[48,1024]{1,0:T(8,128)} %get-tuple-element.341, s32[]{:T(128)S(6)} %select_n.45), kind=kLoop, calls=%fused_computation.5.clone.1 | loop fusion | bytes 98308 | tf_op jit(solution)/shard_map/while/body/eval_jaxpr/dynamic_slice | solution.py:34
  5.9 0.1 shift_right_arithmetic.50
  6.0 0.1 shift_right_arithmetic.51
  6.1 0.1 shift_right_arithmetic.53
  6.2 0.3 fusion.22
  6.5 7.8 %all-gather = f32[128,1024]{1,0:T(8,128)S(1)} all-gather(f32[64,1024]{1,0:T(8,128)S(1)} %get-tuple-element.198), channel_id=2, replica_groups=mesh['hap'=2,'snp'=16] {'hap'}, dimensions={0}, use_global_device_ids=true | all-gather | bytes 786432 | tf_op jit(solution)/shard_map/all_gather | solution.py:97
  14.4 0.1 all_to_all.22
  14.5 15.1 %all_to_all.29 = f32[16,4,1024]{2,1,0:T(4,128)S(1)} all-to-all(f32[16,4,1024]{2,1,0:T(4,128)S(1)} %all_to_all.22), channel_id=1, replica_groups=mesh['hap'=2,'snp'=16] {'snp'}, dimensions={0} | all-to-all | bytes 524288 | tf_op jit(solution)/shard_map/all_to_all | solution.py:98
  29.6 0.3 reduce_sum.61
  29.9 0.3 multiply_reduce_fusion.1
  30.2 0.1 fusion.11
  30.4 9.9 %all_to_all.30 = bf16[4,16,1024]{2,0,1:T(4,128)(2,1)S(1)} all-to-all(bf16[4,16,1024]{2,0,1:T(4,128)(2,1)S(1)} %fusion.11), channel_id=1, replica_groups=mesh['hap'=2,'snp'=16] {'snp'}, dimensions={1} | all-to-all | bytes 262144 | tf_op jit(solution)/shard_map/all_to_all | solution.py:100
  40.3 3.7 %collective-permute-start = (bf16[64,256]{1,0:T(8,128)(2,1)S(1)}, bf16[64,256]{1,0:T(8,128)(2,1)S(1)}, u32[]{:S(2)}, u32[]{:S(2)}) collective-permute-start(bf16[64,256]{1,0:T(8,128)(2,1)S(1)} %get-tuple-element.232), channel_id=1, source_target_pairs={{0,1},{1,2},{2,3},{3,4},{4,5},{5,6},{6,7},{7,8},{8,9},{9,10},{10,1... | collective-permute-start | bytes 98312 | tf_op jit(solution)/shard_map/ppermute | solution.py:14
  44.1 1.9 %collective-permute-start.1 = (bf16[64,256]{1,0:T(8,128)(2,1)S(1)}, bf16[64,256]{1,0:T(8,128)(2,1)S(1)}, u32[]{:S(2)}, u32[]{:S(2)}) collective-permute-start(bf16[64,256]{1,0:T(8,128)(2,1)S(1)} %get-tuple-element.231), channel_id=1, source_target_pairs={{1,0},{2,1},{3,2},{4,3},{5,4},{6,5},{7,6},{8,7},{9,8},{10,9},{11,1... | collective-permute-start | bytes 98312 | tf_op jit(solution)/shard_map/ppermute | solution.py:17
  46.0 4.2 %collective-permute-done.1 = bf16[64,256]{1,0:T(8,128)(2,1)S(1)} collective-permute-done((bf16[64,256]{1,0:T(8,128)(2,1)S(1)}, bf16[64,256]{1,0:T(8,128)(2,1)S(1)}, u32[]{:S(2)}, u32[]{:S(2)}) %collective-permute-start.1) | collective-permute-done | bytes 32800 | tf_op jit(solution)/shard_map/ppermute | solution.py:17
  50.3 0.7 %copy-done.1 = s32[2,1024]{1,0:T(2,128)S(1)} copy-done((s32[2,1024]{1,0:T(2,128)S(1)}, s32[2,1024]{1,0:T(2,128)}, u32[]{:S(2)}) %copy-start.1) | copy-done | bytes 8216
  50.9 6.3 %while.26 = (s32[]{:T(128)}, f32[2,256]{1,0:T(2,128)S(1)}, s32[2]{0:T(128)S(1)}, s32[]{:T(128)}, s32[]{:T(128)}, /*index=5*/s32[2,1024]{1,0:T(2,128)S(1)}, s32[1...) while((s32[]{:T(128)}, f32[2,256]{1,0:T(2,128)S(1)}, ...), condition=%wide.region_9.10_spmd, body=%wide.region_6.9_spmd.sunk | while | flops 28510736 | bytes 194922 | solution.py:91
  50.9 0.6 dynamic_slice.80
  52.3 0.8 %subtract_maximum_fusion.2 = (s32[256]{0:T(256)S(1)}, s32[256]{0:T(256)S(1)}, s32[256]{0:T(256)S(1)}) fusion(s32[256]{0:T(256)S(1)} %bitcast.30, s32[1024]{0:T(1024)} %get-tuple-element.387, s32[]{:T(128)S(6)} %select_n.47, s32[]{:T(128)S(6)} %add.171, s32[256]{0:T(256)S(1)} %bitcast.29), kind=kLoop, calls=%fused_computation.20.clone.1 | loop fusion | flops 1280 | bytes 6152 | tf_op jit(solution)/shard_map/while/body/eval_jaxpr/max | solution.py:79
  53.0 0.1 dynamic-slice_multiply_fusion.2
  53.1 0.1 dynamic_slice.81
  53.2 0.5 fusion.26
  53.7 0.3 convert_reduce_fusion.2
  54.1 0.6 %dynamic_slice.80 = s32[1]{0:T(128)} dynamic-slice(s32[2]{0:T(128)S(1)} %get-tuple-element.383, s32[]{:T(128)} %get-tuple-element.364), dynamic_slice_sizes={1} | dynamic-slice | bytes 12 | tf_op jit(solution)/shard_map/while/body/jit(dynamic_index_in_dim)/dynamic_slice | solution.py:91
  55.4 0.8 %subtract_maximum_fusion.2 = (s32[256]{0:T(256)S(1)}, s32[256]{0:T(256)S(1)}, s32[256]{0:T(256)S(1)}) fusion(s32[256]{0:T(256)S(1)} %bitcast.30, s32[1024]{0:T(1024)} %get-tuple-element.387, s32[]{:T(128)S(6)} %select_n.47, s32[]{:T(128)S(6)} %add.171, s32[256]{0:T(256)S(1)} %bitcast.29), kind=kLoop, calls=%fused_computation.20.clone.1 | loop fusion | flops 1280 | bytes 6152 | tf_op jit(solution)/shard_map/while/body/eval_jaxpr/max | solution.py:79
  56.2 0.1 dynamic-slice_multiply_fusion.2
  56.3 0.1 dynamic_slice.81
  56.4 0.5 fusion.26
  56.9 0.3 convert_reduce_fusion.2
  57.3 3.2 %all-gather.1 = f32[2,1,512]{2,1,0:T(1,128)S(1)} all-gather(f32[1,1,512]{2,1,0:T(1,128)S(1)} %reshape.98), channel_id=1, replica_groups=mesh['hap'=2,'snp'=16] {'hap'}, dimensions={0}, use_global_device_ids=true | all-gather | bytes 6144 | tf_op jit(solution)/shard_map/all_gather | solution.py:116
  60.5 0.6 copy.22
  (33 shorter events, 0.4 us)
Async XLA Ops:
  0.0 0.9 %copy-start = (bf16[64,624]{1,0:T(8,128)(2,1)S(1)}, bf16[64,624]{1,0:T(8,128)(2,1)}, u32[]{:S(2)}) copy-start(bf16[64,624]{1,0:T(8,128)(2,1)} %param.9) | copy-start | bytes 239620
  40.3 5.7 %collective-permute-start = (bf16[64,256]{1,0:T(8,128)(2,1)S(1)}, bf16[64,256]{1,0:T(8,128)(2,1)S(1)}, u32[]{:S(2)}, u32[]{:S(2)}) collective-permute-start(bf16[64,256]{1,0:T(8,128)(2,1)S(1)} %get-tuple-element.232), channel_id=1, source_target_pairs={{0,1},{1,2},{2,3},{3,4},{4,5},{5,6},{6,7},{7,8},{8,9},{9,10},{10,1... | collective-permute-start | bytes 98312 | tf_op jit(solution)/shard_map/ppermute | solution.py:14
  44.1 6.1 %collective-permute-start.1 = (bf16[64,256]{1,0:T(8,128)(2,1)S(1)}, bf16[64,256]{1,0:T(8,128)(2,1)S(1)}, u32[]{:S(2)}, u32[]{:S(2)}) collective-permute-start(bf16[64,256]{1,0:T(8,128)(2,1)S(1)} %get-tuple-element.231), channel_id=1, source_target_pairs={{1,0},{2,1},{3,2},{4,3},{5,4},{6,5},{7,6},{8,7},{9,8},{10,9},{11,1... | collective-permute-start | bytes 98312 | tf_op jit(solution)/shard_map/ppermute | solution.py:17
  50.2 0.7 %copy-start.1 = (s32[2,1024]{1,0:T(2,128)S(1)}, s32[2,1024]{1,0:T(2,128)}, u32[]{:S(2)}) copy-start(s32[2,1024]{1,0:T(2,128)} %param.10) | copy-start | bytes 24580
